TPU v7x, 32 devices: a whole 2x2x4 slice. The times are simulated.
32 devices in a mesh: section: 8 (over z, x), dp: 4 (over y, core).
Axes of the slice: x: 2, y: 2, z: 4, core: 2. Of those that a mesh axis runs over, the one named last changes fastest.
Arguments:
- act_in: bfloat16 [8, 128, 2048], P('section', None, 'dp'), may hold values from -6 to 6
- saved_act: bfloat16 [8, 128, 2048], P('section', None, 'dp'), may hold values from -6 to 6
- cotangent: bfloat16 [8, 128, 2048], P('section', None, 'dp'), may hold values from -6 to 6
- weight_xz: bfloat16 [8, 2048, 8192], P('section', 'dp'), may hold values from -0.125 to 0.125
- weight_bcdt: bfloat16 [8, 320, 2048], P('section', None, 'dp'), may hold values from -0.125 to 0.125
- weight_out: bfloat16 [8, 4096, 2048], P('section', None, 'dp'), may hold values from -0.09375 to 0.09375
- conv_x: float32 [8, 4, 4096], P('section', None, 'dp'), may hold values from -3 to 3
- conv_bc: float32 [8, 4, 256], P('section'), may hold values from -3 to 3
- dt_bias: float32 [8, 64], P('section', 'dp'), may hold values from -8 to -2
- a_log: float32 [8, 64], P('section', 'dp'), may hold values from 0 to 2.7
- d_skip: float32 [8, 64], P('section', 'dp'), may hold values from 0.5 to 1.5
- norm_gain: float32 [8, 4096], P('section', 'dp'), may hold values from 0.1 to 1.9
Outputs:
- next_act: bfloat16 [8, 128, 2048], P('section', None, 'dp')
- prev_grad: bfloat16 [8, 128, 2048], P('section', None, 'dp')
- grad_xz: float32 [8, 2048, 8192], P('section', 'dp')
- grad_bcdt: float32 [8, 320, 2048], P('section', None, 'dp')
- grad_out: float32 [8, 4096, 2048], P('section', None, 'dp')
All inputs are finite; a program needn't handle non-finite values.
Results may differ from a plain program's by a relative error of at most 0.0084.
Values may be sent and summed in bfloat16 or wider, within the bound.
A program may use at most 128 MiB of HBM per device.

v0:
```python
import jax
import jax.numpy as jnp
from jax import lax
from jax.sharding import PartitionSpec as P

D = 2048
HEAD_DIM = 64
NSTATE = 128
HEADS = 64
SEQ = 128
INNER = 4096


def from_behind(x, axis, by):
    length = lax.axis_size(axis)
    return lax.ppermute(x, axis, [(i, (i + by) % length) for i in range(length)])


def causal_conv(values, kernel_taps):
    kernel = kernel_taps.shape[0]
    length = values.shape[1]
    padded = jnp.pad(values, ((0, 0), (kernel - 1, 0), (0, 0)))
    running = jnp.zeros_like(values)
    for offset in range(kernel):
        running = running + kernel_taps[offset] * padded[:, offset : offset + length]
    return running


def map_scores(maps):
    input_map = maps[:, :, :NSTATE]
    output_map = maps[:, :, NSTATE:]
    return lax.dot_general(
        output_map, input_map, (((2,), (2,)), ((0,), (0,))), preferred_element_type=jnp.float32
    )


def map_grads(d_scores, maps):
    values = maps.astype(jnp.float32)
    input_map = values[:, :, :NSTATE]
    output_map = values[:, :, NSTATE:]
    d_input = jnp.einsum("bts,btn->bsn", d_scores, output_map, precision=lax.Precision.HIGHEST)
    d_output = jnp.einsum("bts,bsn->btn", d_scores, input_map, precision=lax.Precision.HIGHEST)
    return jnp.concatenate([d_input, d_output], axis=2)


def mixer(proj_x, proj_z, proj_dt, scores, conv_taps, dt_offset, log_rate, skip_gain):
    batch, length, width = proj_x.shape
    nheads = dt_offset.shape[0]
    head_width = width // nheads
    xconv = jax.nn.silu(causal_conv(proj_x, conv_taps))
    steps = jax.nn.softplus(proj_dt + dt_offset)
    cumul = jnp.cumsum(steps * -jnp.exp(log_rate), axis=1)
    position = jnp.arange(length)
    causal = (position[:, None] >= position[None, :])[None, None]
    heads_cum = jnp.swapaxes(cumul, 1, 2)
    spread = heads_cum[:, :, :, None] - heads_cum[:, :, None, :]
    decay = jnp.where(causal, jnp.exp(jnp.where(causal, spread, 0.0)), 0.0)
    weights = decay * scores[:, None] * jnp.swapaxes(steps, 1, 2)[:, :, None, :]
    heads_in = xconv.reshape(batch, length, nheads, head_width)
    result = jnp.einsum("bhts,bshp->bthp", weights, heads_in, precision=lax.Precision.HIGHEST)
    result = result + skip_gain[None, None, :, None] * heads_in
    gate_in = jax.nn.silu(proj_z.reshape(batch, length, nheads, head_width))
    return (result * gate_in).reshape(batch * length, width)


def times_transposed(left, right):
    return lax.dot_general(
        left, right, (((1,), (1,)), ((), ())), preferred_element_type=jnp.float32
    )


def transposed_times(left, right):
    return lax.dot_general(
        left, right, (((0,), (0,)), ((), ())), preferred_element_type=jnp.float32
    )


def feature_sum(values):
    return lax.psum(jnp.sum(values, axis=1), "dp")


def gate_sum(values):
    return lax.psum(jnp.sum(values, axis=1), "dp")


def send_along(row_block, direction):
    return from_behind(row_block, "section", direction)


def per_device(
    act_in,
    saved_act,
    cotangent,
    weight_xz,
    weight_bcdt,
    weight_out,
    conv_x,
    conv_bc,
    dt_bias,
    a_log,
    d_skip,
    norm_gain,
):
    input_rows = act_in[0]
    saved_rows = saved_act[0]
    cot_rows = cotangent[0]
    local_xz = weight_xz[0]
    local_bcdt = weight_bcdt[0]
    local_out = weight_out[0]
    taps_x = conv_x[0]
    taps_bc = conv_bc[0]
    dt_offset = dt_bias[0]
    log_rate = a_log[0]
    skip_gain = d_skip[0]
    gain_local = norm_gain[0]
    own_heads = dt_offset.shape[0]
    head_first = lax.axis_index("dp") * own_heads
    map_cols = 2 * NSTATE

    def whole_act(pre_part):
        batches = pre_part.shape[0] // SEQ
        conv_in = pre_part.reshape(batches, SEQ, map_cols)
        return jax.nn.silu(causal_conv(conv_in, taps_bc)).reshape(pre_part.shape)

    def project(rows):
        values = rows.astype(jnp.float32)
        scales = lax.rsqrt(feature_sum(values * values)[:, None] / D + 1e-05)
        normed = (values * scales).astype(jnp.bfloat16)
        part_xz = jnp.dot(normed, local_xz, preferred_element_type=jnp.float32)
        part_bcdt = times_transposed(normed, local_bcdt)
        own_xz = lax.psum_scatter(part_xz, "dp", scatter_dimension=1, tiled=True)
        whole_cols = lax.psum(part_bcdt, "dp")
        pre_part = whole_cols[:, :map_cols]
        maps = whole_act(pre_part).astype(jnp.bfloat16)
        own_dt = lax.dynamic_slice_in_dim(whole_cols[:, map_cols:], head_first, own_heads, 1)
        return (values, normed, scales, own_xz, pre_part, maps, own_dt)

    def gate_parts(projected):
        own_xz = projected[3]
        maps = projected[5]
        own_dt = projected[6]
        batches = own_xz.shape[0] // SEQ
        width = own_heads * HEAD_DIM
        split_xz = own_xz.reshape(batches, SEQ, own_heads, 2, HEAD_DIM)
        mix_x = split_xz[:, :, :, 0].reshape(batches, SEQ, width)
        mix_z = split_xz[:, :, :, 1].reshape(batches, SEQ, width)
        maps_three = maps.reshape(batches, SEQ, map_cols)
        scores = map_scores(maps_three)

        def local_mix(in_x, in_z, in_dt, in_scores):
            return mixer(in_x, in_z, in_dt, in_scores, taps_x, dt_offset, log_rate, skip_gain)

        gated, mix_back = jax.vjp(
            local_mix, mix_x, mix_z, own_dt.reshape(batches, SEQ, own_heads), scores
        )
        inverse = lax.rsqrt(gate_sum(gated * gated)[:, None] / INNER + 1e-05)
        mixed_in = (gated * inverse * gain_local).astype(jnp.bfloat16)
        return (gated, mix_back, inverse, mixed_in, maps_three)

    forward_proj = project(input_rows)
    back_proj = project(saved_rows)
    forward_mixed = gate_parts(forward_proj)[3]
    mixed = jnp.dot(
        lax.all_gather(forward_mixed, "dp", axis=1, tiled=True),
        local_out,
        preferred_element_type=jnp.float32,
    )
    section_out = (input_rows.astype(jnp.float32) + mixed).astype(jnp.bfloat16)
    next_act = send_along(section_out, 1)
    values, normed, scales, own_xz, pre_part, maps, own_dt = back_proj
    gated, mix_back, inverse, mixed_in, maps_three = gate_parts(back_proj)
    row_count = values.shape[0]
    grad_out = transposed_times(lax.all_gather(mixed_in, "dp", axis=1, tiled=True), cot_rows)
    d_mixed = lax.psum_scatter(
        times_transposed(cot_rows, local_out), "dp", scatter_dimension=1, tiled=True
    )
    dots = gate_sum(d_mixed * gain_local * gated)
    d_gated = (
        inverse * gain_local * d_mixed
        - gated * (inverse * inverse * inverse) * dots[:, None] / INNER
    )
    d_px, d_pz, d_pdt, d_scores = mix_back(d_gated)
    d_maps = map_grads(d_scores, maps_three).reshape(row_count, map_cols)
    d_dt_full = lax.dynamic_update_slice_in_dim(
        jnp.zeros((row_count, HEADS), jnp.float32),
        d_pdt.reshape(row_count, own_heads),
        head_first,
        1,
    )
    map_part = jnp.concatenate([d_maps, d_dt_full], axis=1)
    summed = lax.psum(map_part, "dp")
    conv_out, conv_back = jax.vjp(whole_act, pre_part)
    d_pre = conv_back(summed[:, :map_cols])[0]
    round_bcdt = jnp.concatenate([d_pre, summed[:, map_cols:]], axis=1).astype(jnp.bfloat16)
    own_round = (
        jnp.stack(
            [
                d_px.reshape(row_count, own_heads, HEAD_DIM),
                d_pz.reshape(row_count, own_heads, HEAD_DIM),
            ],
            axis=2,
        )
        .reshape(row_count, own_heads * 2 * HEAD_DIM)
        .astype(jnp.bfloat16)
    )
    round_xz = lax.all_gather(own_round, "dp", axis=1, tiled=True)
    grad_xz = transposed_times(normed, round_xz)
    grad_bcdt = transposed_times(round_bcdt, normed)
    d_normed = times_transposed(round_xz, local_xz)
    d_normed = d_normed + jnp.dot(round_bcdt, local_bcdt, preferred_element_type=jnp.float32)
    inner_sum = feature_sum(d_normed * values)[:, None]
    d_norm_in = scales * d_normed - values * (scales * scales * scales) * inner_sum / D
    d_input = (cot_rows.astype(jnp.float32) + d_norm_in).astype(jnp.bfloat16)
    prev_grad = send_along(d_input, -1)
    return (next_act[None], prev_grad[None], grad_xz[None], grad_bcdt[None], grad_out[None])


def solution(mesh):
    return jax.shard_map(
        per_device,
        mesh=mesh,
        in_specs=(
            P("section", None, "dp"),
            P("section", None, "dp"),
            P("section", None, "dp"),
            P("section", "dp", None),
            P("section", None, "dp"),
            P("section", None, "dp"),
            P("section", None, "dp"),
            P("section", None, None),
            P("section", "dp"),
            P("section", "dp"),
            P("section", "dp"),
            P("section", "dp"),
        ),
        out_specs=(
            P("section", None, "dp"),
            P("section", None, "dp"),
            P("section", "dp", None),
            P("section", None, "dp"),
            P("section", None, "dp"),
        ),
        check_vma=False,
    )
```

profile of v0, /device:TPU:0, one launch (start us, length us, event | category | flops | bytes accessed | tf_op | source)
XLA Modules:
  0.0 311.2 jit_solution(6612498661934579519)
XLA Ops:
  8.3 8.4 %psum.66 = f32[128]{0:T(128)S(1)} all-reduce(f32[128]{0:T(128)S(1)} %fusion.86), channel_id=1, replica_groups=mesh['section'=8,'dp'=4] {'dp'}, use_global_device_ids=true, to_apply=%region_8.9 | all-reduce | flops 128 | bytes 1024 | tf_op jit(solution)/shard_map/psum | solution.py:79
  17.2 1.9 fusion.80
  19.2 6.8 %fusion.2 = f32[128,8192]{1,0:T(8,128)} fusion(bf16[1,512,8192]{2,1,0:T(8,128)(2,1)} %param.15, bf16[1,128,512]{2,1,0:T(8,128)(2,1)} %param.13, f32[128]{0:T(128)S(1)} %get-tuple-element.49), kind=kOutput, calls=%fused_computation.3 | convolution fusion | flops 1073938432 | bytes 12714496 | tf_op jit(solution)/shard_map/dot_general | solution.py:129
  26.9 5.0 %fusion.6 = f32[128,4096]{1,0:T(8,128)} fusion(bf16[1,4096,512]{2,1,0:T(8,128)(2,1)} %param.17, bf16[1,128,512]{2,1,0:T(8,128)(2,1)S(1)} %copy-done.5), kind=kOutput, calls=%fused_computation.8 | convolution fusion | flops 536870912 | bytes 6422528 | tf_op jit(solution)/shard_map/dot_general | solution.py:67
  32.2 19.0 %all-reduce.18.cloned.1.call-done = f32[128,320]{0,1:T(8,128)} async-done(((f32[128,320]{0,1:T(8,128)}), f32[128,320]{0,1:T(8,128)}) %all-reduce.18.cloned.1.call-update) | async-done | bytes 163856 | tf_op jit(solution)/shard_map/psum | solution.py:132
  53.3 1.9 multiply_convert_fusion.2
  55.4 43.6 %reduce-scatter.6.cloned.1.call-done = f32[128,2048]{1,0:T(8,128)} async-done(((f32[128,8192]{1,0:T(8,128)}), f32[128,2048]{1,0:T(8,128)}) %reduce-scatter.6.cloned.1.call-update) | async-done | bytes 1048592 | tf_op jit(solution)/shard_map/reduce_scatter | solution.py:131
  99.0 1.5 copy.55
  101.8 3.0 multiply_reduce_fusion.3
  104.8 1.2 copy.60
  106.1 27.5 %reduce-scatter.8.cloned.1.call-done = f32[128,1024]{1,0:T(8,128)} async-done(((f32[128,4096]{1,0:T(8,128)}), f32[128,1024]{1,0:T(8,128)}) %reduce-scatter.8.cloned.1.call-update) | async-done | bytes 524304 | tf_op jit(solution)/shard_map/reduce_scatter | solution.py:174
  134.7 5.8 %all-reduce.13 = (f32[128]{0:T(128)S(1)}, f32[128]{0:T(128)S(1)}, f32[128]{0:T(128)S(1)}) all-reduce(f32[128]{0:T(128)S(1)} %fusion.84, f32[128]{0:T(128)S(1)} %multiply_reduce_fusion.2, f32[128]{0:T(128)S(1)} %get-tuple-element.20), channel_id=1, replica_groups=mesh['section'=8,'dp'=4] {'dp'}, use_global_device_ids=true, to_apply=%region_1.0 | all-reduce | flops 384 | bytes 3072 | tf_op jit(solution)/shard_map/psum | solution.py:79
  140.5 6.7 %fusion.4 = f32[128,8192]{1,0:T(8,128)} fusion(bf16[1,512,8192]{2,1,0:T(8,128)(2,1)} %param.15, bf16[1,128,512]{2,1,0:T(8,128)(2,1)S(1)} %copy-done.3, f32[128]{0:T(128)S(1)} %add_rsqrt_fusion.3), kind=kOutput, calls=%fused_computation.5 | convolution fusion | flops 1073938432 | bytes 12714496 | tf_op jit(solution)/shard_map/dot_general | solution.py:129
  147.5 2.0 multiply_convert_fusion
  149.7 4.2 %fusion.32 = (f32[16,128]{1,0:T(8,128)S(1)}, f32[16,128]{1,0:T(8,128)S(1)}, f32[16,128]{1,0:T(8,128)}, f32[128,128]{1,0:T(8,128)S(1)}) fusion(f32[16,128]{1,0:T(8,128)S(1)} %get-tuple-element.37, f32[128,128]{1,0:T(8,128)S(1)} %fusion.125, f32[16,128]{1,0:T(8,128)S(1)} %copy.57, pred[128,128]{1,0:T(8,128)(4,1)S(1)} %iota_compare_fusion, ...), kind=kOutput, calls=%fused_computation.47 | convolution fusion | flops 205891584 | bytes 1769472 | tf_op jit(solution)/shard_map/transpose(jvp(bhts,bshp->bthp))/dot_general | solution.py:60
  157.2 1.7 fusion.82
  159.1 2.3 fusion.10
  161.7 31.3 %reduce-scatter.4.cloned.1.call-done = f32[128,2048]{1,0:T(8,128)} async-done(((f32[128,8192]{1,0:T(8,128)}), f32[128,2048]{1,0:T(8,128)}) %reduce-scatter.4.cloned.1.call-update) | async-done | bytes 1048592 | tf_op jit(solution)/shard_map/reduce_scatter | solution.py:131
  193.0 1.5 copy.49
  194.6 1.9 broadcast_multiply_fusion.1
  198.9 28.8 %all-reduce.20.cloned.1.call-done = (f32[128,320]{0,1:T(8,128)}, f32[128,320]{0,1:T(8,128)}) async-done(((f32[128,320]{0,1:T(8,128)}, f32[128,320]{0,1:T(8,128)}), (f32[128,320]{0,1:T(8,128)}, f32[128,320]{0,1:T(8,128)})) %all-reduce.20.cloned.1.call-update) | async-done | bytes 327696 | tf_op jit(solution)/shard_map/psum | solution.py:132
  233.2 3.3 %multiply_reduce_fusion.4 = (f32[128]{0:T(128)S(1)}, f32[1,128,16,64]{1,3,2,0:T(8,128)S(1)}) fusion(f32[1,128,16,2,64]{1,4,3,2,0:T(8,128)S(1)} %bitcast.276, f32[1,128,16,64]{1,3,2,0:T(8,128)} %bitcast.288, f32[16]{0:T(128)S(1)} %bitcast.320, f32[128,16,64]{0,2,1:T(8,128)} %bitcast.289, f32[16,128]{1,0:T(8,128)S(1)} %get-tuple-element.35, ...), kind=kOutput, calls=%fused_computation.94 | convolution fusion | flops 203816832 | bytes 2204672 | tf_op jit(solution)/shard_map/jvp(bhts,bshp->bthp)/dot_general | solution.py:60
  236.8 15.6 %all-gather.6.cloned.1.call-done = bf16[128,8192]{0,1:T(8,128)(2,1)} async-done(((bf16[128,2048]{0,1:T(8,128)(2,1)}), bf16[128,8192]{0,1:T(8,128)(2,1)}) %all-gather.6.cloned.1.call-update) | async-done | bytes 2097168 | tf_op jit(solution)/shard_map/all_gather | solution.py:206
  252.3 6.9 %fusion = f32[128,512]{1,0:T(8,128)S(1)} fusion(bf16[128,8192]{0,1:T(8,128)(2,1)} %all-gather.6.cloned.1.call-done, bf16[1,512,8192]{2,1,0:T(8,128)(2,1)} %param.15), kind=kOutput, calls=%fused_computation.1 | convolution fusion | flops 1073741824 | bytes 10747904 | tf_op jit(solution)/shard_map/dot_general | solution.py:67
  259.6 6.3 %all-reduce.12 = (f32[128]{0:T(128)S(1)}, f32[128]{0:T(128)S(1)}) all-reduce(f32[128]{0:T(128)S(1)} %get-tuple-element.53, f32[128]{0:T(128)S(1)} %get-tuple-element.55), channel_id=1, replica_groups=mesh['section'=8,'dp'=4] {'dp'}, use_global_device_ids=true, to_apply=%region_6.7 | all-reduce | flops 256 | bytes 2048 | tf_op jit(solution)/shard_map/psum | solution.py:83
  267.9 3.4 %all-gather.8.cloned.1.call-done = bf16[128,4096]{1,0:T(8,128)(2,1)} async-done(((bf16[128,1024]{1,0:T(8,128)(2,1)}), bf16[128,4096]{1,0:T(8,128)(2,1)}) %all-gather.8.cloned.1.call-update) | async-done | bytes 1048592 | tf_op jit(solution)/shard_map/all_gather | solution.py:173
  271.3 5.9 %convolution_bitcast_fusion.1 = f32[1,4096,512]{2,1,0:T(8,128)} fusion(bf16[128,4096]{1,0:T(8,128)(2,1)} %all-gather.8.cloned.1.call-done, bf16[1,128,512]{2,1,0:T(8,128)(2,1)S(1)} %copy-done.5), kind=kOutput, calls=%fused_computation.7 | convolution fusion | flops 536870912 | bytes 9568256 | tf_op jit(solution)/shard_map/dot_general | solution.py:73
  277.4 4.3 %collective-permute-start.1 = (bf16[128,512]{1,0:T(8,128)(2,1)S(1)}, bf16[128,512]{1,0:T(8,128)(2,1)S(1)}, u32[]{:S(2)}, u32[]{:S(2)}) collective-permute-start(bf16[128,512]{1,0:T(8,128)(2,1)S(1)} %fusion.91), channel_id=1, source_target_pairs={{0,28},{4,0},{8,4},{12,8},{16,12},{20,16},{24,20},{28,24},{1,29},{... | collective-permute-start | bytes 393224 | tf_op jit(solution)/shard_map/ppermute | solution.py:16
  281.7 8.0 %all-gather.4.cloned.1.call-done = bf16[128,4096]{1,0:T(8,128)(2,1)} async-done(((bf16[128,1024]{1,0:T(8,128)(2,1)}), bf16[128,4096]{1,0:T(8,128)(2,1)}) %all-gather.4.cloned.1.call-update) | async-done | bytes 1048592 | tf_op jit(solution)/shard_map/all_gather | solution.py:164
  289.7 3.2 %fusion.17 = bf16[128,512]{1,0:T(8,128)(2,1)S(1)} fusion(bf16[128,4096]{1,0:T(8,128)(2,1)} %all-gather.4.cloned.1.call-done, bf16[1,4096,512]{2,1,0:T(8,128)(2,1)} %param.17, bf16[1,128,512]{2,1,0:T(8,128)(2,1)S(1)} %copy-done.4), kind=kOutput, calls=%fused_computation.28 | convolution fusion | flops 537067520 | bytes 5505024 | tf_op jit(solution)/shard_map/dot_general | solution.py:163
  292.9 1.5 collective-permute-start
  294.4 8.6 %convolution_bitcast_fusion = f32[1,512,8192]{2,1,0:T(8,128)} fusion(bf16[128,8192]{0,1:T(8,128)(2,1)S(1)} %copy-done.1, bf16[1,128,512]{2,1,0:T(8,128)(2,1)S(1)} %copy-done.2, f32[128]{0:T(128)S(1)} %get-tuple-element.49), kind=kOutput, calls=%fused_computation | convolution fusion | flops 1073938432 | bytes 19005952 | tf_op jit(solution)/shard_map/dot_general | solution.py:73
  (131 shorter events, 23.6 us)
Async XLA Ops:
  7.2 10.1 %copy-start = (bf16[1,320,512]{2,1,0:T(8,128)(2,1)S(1)}, bf16[1,320,512]{2,1,0:T(8,128)(2,1)}, u32[]{:S(2)}) copy-start(bf16[1,320,512]{2,1,0:T(8,128)(2,1)} %param.16) | copy-start | bytes 983044
  7.2 44.0 %all-reduce.18.cloned.1.call-start = ((), (), s32[]{:S(2)}) async-start(), calls=%async_computation.6 | async-start | bytes 327680 | tf_op jit(solution)/shard_map/psum | solution.py:132
  19.2 79.8 %reduce-scatter.6.cloned.1.call-start = ((), (), s32[]{:S(2)}) async-start(), calls=%async_computation.5 | async-start | bytes 5242880 | tf_op jit(solution)/shard_map/reduce_scatter | solution.py:131
  26.1 25.9 %copy-start.19 = (f32[1,16]{1,0:T(1,128)S(1)}, f32[1,16]{1,0:T(1,128)}, u32[]{:S(2)}) copy-start(f32[1,16]{1,0:T(1,128)} %param.20) | copy-start | bytes 196
  26.1 107.5 %reduce-scatter.8.cloned.1.call-start = ((), (), s32[]{:S(2)}) async-start(), calls=%async_computation.7 | async-start | bytes 2621440 | tf_op jit(solution)/shard_map/reduce_scatter | solution.py:174
  31.9 69.9 %copy-start.27 = (f32[1,16]{1,0:T(1,128)S(1)}, f32[1,16]{1,0:T(1,128)}, u32[]{:S(2)}) copy-start(f32[1,16]{1,0:T(1,128)} %param.22) | copy-start | bytes 196
  31.9 161.1 %reduce-scatter.4.cloned.1.call-start = ((), (), s32[]{:S(2)}) async-start(), calls=%async_computation.3 | async-start | bytes 5242880 | tf_op jit(solution)/shard_map/reduce_scatter | solution.py:131
  32.1 21.2 %copy-start.21 = (f32[16]{0:T(128)}, f32[16]{0:T(128)S(1)}, u32[]{:S(2)}) copy-start(f32[16]{0:T(128)S(1)} %negate_bitcast_fusion) | copy-start | bytes 196
  32.2 68.4 %copy-start.13 = (f32[1,1,256]{2,1,0:T(1,128)}, f32[1,1,256]{2,1,0:T(1,128)S(1)}, u32[]{:S(2)}) copy-start(f32[1,1,256]{2,1,0:T(1,128)S(1)} %get-tuple-element.44) | copy-start | bytes 3076
  32.2 72.6 %copy-start.15 = (f32[1,1,256]{2,1,0:T(1,128)}, f32[1,1,256]{2,1,0:T(1,128)S(1)}, u32[]{:S(2)}) copy-start(f32[1,1,256]{2,1,0:T(1,128)S(1)} %get-tuple-element.46) | copy-start | bytes 3076
  52.0 97.6 %copy-start.17 = (f32[16,128]{1,0:T(8,128)}, f32[16,128]{1,0:T(8,128)S(1)}, u32[]{:S(2)}) copy-start(f32[16,128]{1,0:T(8,128)S(1)} %get-tuple-element.37) | copy-start | bytes 24580
  52.4 97.3 %copy-start.18 = (f32[16,128]{1,0:T(8,128)}, f32[16,128]{1,0:T(8,128)S(1)}, u32[]{:S(2)}) copy-start(f32[16,128]{1,0:T(8,128)S(1)} %copy.57) | copy-start | bytes 24580
  55.4 94.3 %copy-start.10 = (f32[128,128]{1,0:T(8,128)}, f32[128,128]{1,0:T(8,128)S(1)}, u32[]{:S(2)}) copy-start(f32[128,128]{1,0:T(8,128)S(1)} %fusion.125) | copy-start | bytes 196612
  100.6 33.0 %copy-start.11 = (f32[1,1024]{1,0:T(1,128)S(1)}, f32[1,1024]{1,0:T(1,128)}, u32[]{:S(2)}) copy-start(f32[1,1024]{1,0:T(1,128)} %param.23) | copy-start | bytes 12292
  101.8 45.4 %copy-start.8 = (f32[1,128,1024]{1,2,0:T(8,128)}, f32[1,128,1024]{1,2,0:T(8,128)S(1)}, u32[]{:S(2)}) copy-start(f32[1,128,1024]{1,2,0:T(8,128)S(1)} %get-tuple-element.24) | copy-start | bytes 1572868
  147.3 80.4 %all-reduce.20.cloned.1.call-start = ((), (), s32[]{:S(2)}) async-start(), calls=%async_computation.10 | async-start | bytes 655360 | tf_op jit(solution)/shard_map/psum | solution.py:132
  161.7 90.6 %all-gather.6.cloned.1.call-start = ((), (), s32[]{:S(2)}) async-start(), calls=%async_computation.8 | async-start | bytes 2621440 | tf_op jit(solution)/shard_map/all_gather | solution.py:206
  194.6 35.5 %copy-start.9 = (f32[1,128,256]{1,2,0:T(8,128)S(1)}, f32[1,128,256]{1,2,0:T(8,128)}, u32[]{:S(2)}) copy-start(f32[1,128,256]{1,2,0:T(8,128)} %get-tuple-element.23) | copy-start | bytes 393220
  194.6 36.5 %copy-start.14 = (f32[1,1,256]{2,1,0:T(1,128)S(1)}, f32[1,1,256]{2,1,0:T(1,128)}, u32[]{:S(2)}) copy-start(f32[1,1,256]{2,1,0:T(1,128)} %copy-done.13) | copy-start | bytes 3076
  194.6 36.5 %copy-start.16 = (f32[1,1,256]{2,1,0:T(1,128)S(1)}, f32[1,1,256]{2,1,0:T(1,128)}, u32[]{:S(2)}) copy-start(f32[1,1,256]{2,1,0:T(1,128)} %copy-done.15) | copy-start | bytes 3076
  196.5 36.1 %copy-start.20 = (f32[1,16]{1,0:T(1,128)S(1)}, f32[1,16]{1,0:T(1,128)}, u32[]{:S(2)}) copy-start(f32[1,16]{1,0:T(1,128)} %param.20) | copy-start | bytes 196
  196.5 36.1 %copy-start.22 = (f32[16]{0:T(128)S(1)}, f32[16]{0:T(128)}, u32[]{:S(2)}) copy-start(f32[16]{0:T(128)} %copy-done.21) | copy-start | bytes 196
  196.5 36.7 %copy-start.28 = (f32[1,16]{1,0:T(1,128)S(1)}, f32[1,16]{1,0:T(1,128)}, u32[]{:S(2)}) copy-start(f32[1,16]{1,0:T(1,128)} %param.22) | copy-start | bytes 196
  197.9 73.4 %all-gather.8.cloned.1.call-start = ((), (), s32[]{:S(2)}) async-start(), calls=%async_computation.9 | async-start | bytes 1310720 | tf_op jit(solution)/shard_map/all_gather | solution.py:173
  198.6 91.0 %all-gather.4.cloned.1.call-start = ((), (), s32[]{:S(2)}) async-start(), calls=%async_computation.4 | async-start | bytes 1310720 | tf_op jit(solution)/shard_map/all_gather | solution.py:164
  236.7 22.5 %copy-start.2 = (bf16[1,128,512]{2,1,0:T(8,128)(2,1)S(1)}, bf16[1,128,512]{2,1,0:T(8,128)(2,1)}, u32[]{:S(2)}) copy-start(bf16[1,128,512]{2,1,0:T(8,128)(2,1)} %param.13) | copy-start | bytes 393220
  267.9 9.3 %copy-start.6 = (bf16[1,128,512]{2,1,0:T(8,128)(2,1)S(1)}, bf16[1,128,512]{2,1,0:T(8,128)(2,1)}, u32[]{:S(2)}) copy-start(bf16[1,128,512]{2,1,0:T(8,128)(2,1)} %param.14) | copy-start | bytes 393220
  267.9 9.3 %copy-start.25 = (f32[128]{0:T(128)S(1)}, f32[128]{0:T(128)}, u32[]{:S(2)}) copy-start(f32[128]{0:T(128)} %get-tuple-element.48) | copy-start | bytes 1540
  267.9 21.8 %copy-start.4 = (bf16[1,128,512]{2,1,0:T(8,128)(2,1)S(1)}, bf16[1,128,512]{2,1,0:T(8,128)(2,1)}, u32[]{:S(2)}) copy-start(bf16[1,128,512]{2,1,0:T(8,128)(2,1)} %param.12) | copy-start | bytes 393220
  277.2 17.2 %copy-start.1 = (bf16[128,8192]{0,1:T(8,128)(2,1)S(1)}, bf16[128,8192]{0,1:T(8,128)(2,1)}, u32[]{:S(2)}) copy-start(bf16[128,8192]{0,1:T(8,128)(2,1)} %all-gather.6.cloned.1.call-done) | copy-start | bytes 6291460
  277.4 25.7 %collective-permute-start.1 = (bf16[128,512]{1,0:T(8,128)(2,1)S(1)}, bf16[128,512]{1,0:T(8,128)(2,1)S(1)}, u32[]{:S(2)}, u32[]{:S(2)}) collective-permute-start(bf16[128,512]{1,0:T(8,128)(2,1)S(1)} %fusion.91), channel_id=1, source_target_pairs={{0,28},{4,0},{8,4},{12,8},{16,12},{20,16},{24,20},{28,24},{1,29},{... | collective-permute-start | bytes 393224 | tf_op jit(solution)/shard_map/ppermute | solution.py:16
  292.9 10.1 %collective-permute-start = (bf16[128,512]{1,0:T(8,128)(2,1)S(1)}, bf16[128,512]{1,0:T(8,128)(2,1)S(1)}, u32[]{:S(2)}, u32[]{:S(2)}) collective-permute-start(bf16[128,512]{1,0:T(8,128)(2,1)S(1)} %fusion.17), channel_id=1, source_target_pairs={{0,4},{4,8},{8,12},{12,16},{16,20},{20,24},{24,28},{28,0},{1,5},{5... | collective-permute-start | bytes 393224 | tf_op jit(solution)/shard_map/ppermute | solution.py:16
  (7 other events, 41.0 us)
Sparse Core Ops, SparseCore 0:
  19.3 31.8 all-reduce.17
  54.4 44.5 reduce-scatter.5
  102.1 31.4 reduce-scatter.7
  147.4 45.5 reduce-scatter.3
  195.2 32.4 all-reduce.19
  229.7 22.5 all-gather.5
  254.4 16.8 all-gather.7
  272.9 16.7 all-gather.3
where the time goes:
time: 312 us; the launch traced here: 311 us
  waiting for transfers between devices  178 us (57%)
  matrix products  61.8 us (20%)
  blocking collectives  20.4 us (7%)
  other arithmetic  17.4 us (6%)
  between operations  14.7 us (5%)
  local copies, waits for them, and re-layouts  12.5 us (4%)
  starting transfers between devices  6.58 us (2%)
    reduce_scatter x2, waiting for transfers between devices, project(): own_xz = lax.psum_scatter(part_xz, 'dp', scatter_dimension=1, tiled=True)  74.9 us
    psum x2, waiting for transfers between devices, project(): whole_cols = lax.psum(part_bcdt, 'dp')  47.7 us
    reduce_scatter x1, waiting for transfers between devices, per_device(): lax.psum_scatter(times_transposed(cot_rows, local_out), 'dp', scatter_dim...  27.5 us
    dot_general x3, matrix products, transposed_times(): lax.dot_general(left, right, (((0,), (0,)), ((), ())), preferred_element_...  15.6 us
    all_gather x1, waiting for transfers between devices, per_device(): round_xz = lax.all_gather(own_round, 'dp', axis=1, tiled=True)  15.6 us
    dot_general x4, matrix products, times_transposed(): lax.dot_general(left, right, (((1,), (1,)), ((), ())), preferred_element_...  15.5 us
    psum x2, blocking collectives, feature_sum(): return lax.psum(jnp.sum(values, axis=1), 'dp')  14.1 us
    dot_general x2, matrix products, project(): part_xz = jnp.dot(normed, local_xz, preferred_element_type=jnp.float32)  13.5 us
  transfers between devices with their start and end apart: 10, of which 8 were waited for; matrix products, arithmetic and copies ran while one was open for 25% of the time, Pallas kernels for 0%

commit v1 on v0

--- a/solution.py
+++ b/solution.py
@@ -1,3 +1,4 @@
+import functools
 import jax
 import jax.numpy as jnp
 from jax import lax
@@ -9,6 +10,18 @@
 HEADS = 64
 SEQ = 128
 INNER = 4096
+
+
+def take_the_rails(work_x, shard_axis):
+    lanes = jax.lax.axis_size(shard_axis)
+    wide_out = lambda formed: [(dev_j, dev_j ^ formed) for dev_j in range(lanes)]
+    b_now = work_x
+    for k0 in range(lanes.bit_length() - 1):
+        b_now = b_now + jax.lax.ppermute(b_now, shard_axis, wide_out(1 << k0))
+    return b_now
+
+
+clear_the_lots_all = functools.partial(take_the_rails, shard_axis="dp")
 
 
 def from_behind(x, axis, by):
@@ -129,7 +142,7 @@
         part_xz = jnp.dot(normed, local_xz, preferred_element_type=jnp.float32)
         part_bcdt = times_transposed(normed, local_bcdt)
         own_xz = lax.psum_scatter(part_xz, "dp", scatter_dimension=1, tiled=True)
-        whole_cols = lax.psum(part_bcdt, "dp")
+        whole_cols = clear_the_lots_all(part_bcdt)
         pre_part = whole_cols[:, :map_cols]
         maps = whole_act(pre_part).astype(jnp.bfloat16)
         own_dt = lax.dynamic_slice_in_dim(whole_cols[:, map_cols:], head_first, own_heads, 1)

time: 312 us -> 281 us (0.901)
  waiting for transfers between devices: 178 us -> 145 us
  other arithmetic: 17.4 us -> 21.5 us
    reduce_scatter x2, waiting for transfers between devices: 74.9 us -> 52.7 us  [project(): own_xz = lax.psum_scatter(part_xz, 'dp', scatter_dimension=1, tiled=True)]
    psum x2 -> x1, waiting for transfers between devices: 47.7 us -> 26.1 us  [per_device(): summed = lax.psum(map_part, 'dp')]
    ppermute x0 -> x4, waiting for transfers between devices: none -> 9.65 us  [take_the_rails(): b_now = b_now + jax.lax.ppermute(b_now, shard_axis, wide_out(1 << k0))]
  transfers between devices with their start and end apart: 10 -> 13, of which waited for: 8 -> 10; matrix products, arithmetic and copies ran while one was open for 25% -> 26% of each run, Pallas kernels for 0% -> 0%
where the time goes in v1:
time: 281 us
  waiting for transfers between devices  145 us (52%)
  matrix products  59.7 us (21%)
  other arithmetic  21.5 us (8%)
  blocking collectives  20.6 us (7%)
  between operations  14.8 us (5%)
  local copies, waits for them, and re-layouts  9.77 us (3%)
  starting transfers between devices  8.99 us (3%)
    reduce_scatter x2, waiting for transfers between devices, project(): own_xz = lax.psum_scatter(part_xz, 'dp', scatter_dimension=1, tiled=True)  52.7 us
    reduce_scatter x1, waiting for transfers between devices, per_device(): lax.psum_scatter(times_transposed(cot_rows, local_out), 'dp', scatter_dim...  26.3 us
    psum x1, waiting for transfers between devices, per_device(): summed = lax.psum(map_part, 'dp')  26.1 us
    all_gather x1, waiting for transfers between devices, per_device(): round_xz = lax.all_gather(own_round, 'dp', axis=1, tiled=True)  18.6 us
    dot_general x3, matrix products, transposed_times(): lax.dot_general(left, right, (((0,), (0,)), ((), ())), preferred_element_...  15.6 us
    psum x2, blocking collectives, feature_sum(): return lax.psum(jnp.sum(values, axis=1), 'dp')  14.3 us
    dot_general x2, matrix products, project(): part_xz = jnp.dot(normed, local_xz, preferred_element_type=jnp.float32)  13.5 us
    dot_general x4, matrix products, times_transposed(): lax.dot_general(left, right, (((1,), (1,)), ((), ())), preferred_element_...  13.2 us
  transfers between devices with their start and end apart: 13, of which 10 were waited for; matrix products, arithmetic and copies ran while one was open for 26% of the time, Pallas kernels for 0%

profile of v1, /device:TPU:0, one launch (start us, length us, event | category | flops | bytes accessed | tf_op | source)
XLA Modules:
  0.0 280.5 jit_solution(5150698043640572512)
XLA Ops:
  8.3 8.4 %psum.51 = f32[128]{0:T(128)S(1)} all-reduce(f32[128]{0:T(128)S(1)} %fusion.86), channel_id=1, replica_groups=mesh['section'=8,'dp'=4] {'dp'}, use_global_device_ids=true, to_apply=%region_7.8 | all-reduce | flops 128 | bytes 1024 | tf_op jit(solution)/shard_map/psum | solution.py:92
  17.2 6.8 %fusion.2 = f32[128,8192]{1,0:T(8,128)} fusion(bf16[1,512,8192]{2,1,0:T(8,128)(2,1)} %param.15, bf16[1,128,512]{2,1,0:T(8,128)(2,1)} %param.13, f32[128]{0:T(128)S(1)} %get-tuple-element.48), kind=kOutput, calls=%fused_computation.3 | convolution fusion | flops 1073938432 | bytes 12714496 | tf_op jit(solution)/shard_map/dot_general | solution.py:142
  24.9 5.0 %fusion.6 = f32[128,4096]{1,0:T(8,128)} fusion(bf16[1,4096,512]{2,1,0:T(8,128)(2,1)} %param.17, bf16[1,128,512]{2,1,0:T(8,128)(2,1)S(1)} %copy-done.5), kind=kOutput, calls=%fused_computation.8 | convolution fusion | flops 536870912 | bytes 6422528 | tf_op jit(solution)/shard_map/dot_general | solution.py:80
  33.2 5.0 %collective-permute-done.4 = f32[128,320]{0,1:T(8,128)S(1)} collective-permute-done((f32[128,320]{0,1:T(8,128)S(1)}, f32[128,320]{0,1:T(8,128)S(1)}, u32[]{:S(2)}, u32[]{:S(2)}) %collective-permute-start.4) | collective-permute-done | bytes 163872 | tf_op jit(solution)/shard_map/ppermute | solution.py:20
  41.0 28.0 %reduce-scatter.6.cloned.1.call-done = f32[128,2048]{1,0:T(8,128)} async-done(((f32[128,8192]{1,0:T(8,128)}), f32[128,2048]{1,0:T(8,128)}) %reduce-scatter.6.cloned.1.call-update) | async-done | bytes 1048592 | tf_op jit(solution)/shard_map/reduce_scatter | solution.py:144
  69.0 1.5 copy.55
  71.9 4.3 %multiply_reduce_fusion.3 = (f32[128]{0:T(128)}, f32[1,128,16,64]{1,3,2,0:T(8,128)}, f32[1,128,16,64]{1,3,2,0:T(8,128)}) fusion(f32[1,128,16,2,64]{1,4,3,2,0:T(8,128)S(1)} %bitcast.271, f32[1,128,16,64]{1,3,2,0:T(8,128)S(1)} %bitcast.283, f32[16]{0:T(128)} %bitcast.317, f32[128,16,64]{0,2,1:T(8,128)S(1)} %bitcast.284, f32[16,128]{1,0:T(8,128)S(1)} %copy-done.30, ...), kind=kOutput, calls=%fused_computation.80 | convolution fusion | flops 203816832 | bytes 2728960 | tf_op jit(solution)/shard_map/jvp(bhts,bshp->bthp)/dot_general | solution.py:73
  77.5 26.3 %reduce-scatter.8.cloned.1.call-done = f32[128,1024]{1,0:T(8,128)} async-done(((f32[128,4096]{1,0:T(8,128)}), f32[128,1024]{1,0:T(8,128)}) %reduce-scatter.8.cloned.1.call-update) | async-done | bytes 524304 | tf_op jit(solution)/shard_map/reduce_scatter | solution.py:187
  104.9 5.9 %all-reduce.13 = (f32[128]{0:T(128)S(1)}, f32[128]{0:T(128)S(1)}, f32[128]{0:T(128)S(1)}) all-reduce(f32[128]{0:T(128)} %fusion.84, f32[128]{0:T(128)S(1)} %multiply_reduce_fusion.2, f32[128]{0:T(128)} %get-tuple-element.18), channel_id=1, replica_groups=mesh['section'=8,'dp'=4] {'dp'}, use_global_device_ids=true, to_apply=%region_1.0 | all-reduce | flops 384 | bytes 3072 | tf_op jit(solution)/shard_map/psum | solution.py:92
  110.8 6.7 %fusion.4 = f32[128,8192]{1,0:T(8,128)} fusion(bf16[1,512,8192]{2,1,0:T(8,128)(2,1)} %param.15, bf16[1,128,512]{2,1,0:T(8,128)(2,1)S(1)} %copy-done.3, f32[128]{0:T(128)S(1)} %add_rsqrt_fusion.3), kind=kOutput, calls=%fused_computation.5 | convolution fusion | flops 1073938432 | bytes 12714496 | tf_op jit(solution)/shard_map/dot_general | solution.py:142
  117.8 2.0 multiply_convert_fusion
  121.1 2.0 fusion.95
  123.1 2.4 fusion.10
  126.5 3.0 %fusion.32 = (f32[16,128]{1,0:T(8,128)S(1)}, f32[16,128]{1,0:T(8,128)S(1)}, f32[16,128]{1,0:T(8,128)}, f32[128,128]{1,0:T(8,128)S(1)}) fusion(f32[16,128]{1,0:T(8,128)S(1)} %copy-done.31, f32[128,128]{1,0:T(8,128)S(1)} %copy-done.12, f32[16,128]{1,0:T(8,128)S(1)} %copy-done.32, pred[128,128]{1,0:T(8,128)(4,1)S(1)} %copy-done.22, ...), kind=kOutput, calls=%fused_computation.47 | convolution fusion | flops 205891584 | bytes 1769472 | tf_op jit(solution)/shard_map/transpose(jvp(bhts,bshp->bthp))/dot_general | solution.py:73
  129.7 1.7 collective-permute-start.1
  133.0 3.4 %collective-permute-done.1 = f32[128,320]{0,1:T(8,128)S(1)} collective-permute-done((f32[128,320]{0,1:T(8,128)S(1)}, f32[128,320]{0,1:T(8,128)S(1)}, u32[]{:S(2)}, u32[]{:S(2)}) %collective-permute-start.1) | collective-permute-done | bytes 163872 | tf_op jit(solution)/shard_map/ppermute | solution.py:20
  136.4 1.5 multiply_bitcast_fusion.1
  138.7 24.7 %reduce-scatter.4.cloned.1.call-done = f32[128,2048]{1,0:T(8,128)} async-done(((f32[128,8192]{1,0:T(8,128)}), f32[128,2048]{1,0:T(8,128)}) %reduce-scatter.4.cloned.1.call-update) | async-done | bytes 1048592 | tf_op jit(solution)/shard_map/reduce_scatter | solution.py:144
  163.4 1.5 copy.49
  165.0 2.6 broadcast_multiply_fusion.1
  171.1 26.1 %all-reduce.16.cloned.1.call-done = f32[128,320]{0,1:T(8,128)} async-done(((f32[128,320]{0,1:T(8,128)}), f32[128,320]{0,1:T(8,128)}) %all-reduce.16.cloned.1.call-update) | async-done | bytes 163856 | tf_op jit(solution)/shard_map/psum | solution.py:204
  199.7 3.3 %multiply_reduce_fusion.4 = (f32[128]{0:T(128)S(1)}, f32[1,128,16,64]{1,3,2,0:T(8,128)S(1)}) fusion(f32[1,128,16,2,64]{1,4,3,2,0:T(8,128)S(1)} %bitcast.276, f32[1,128,16,64]{1,3,2,0:T(8,128)} %bitcast.288, f32[16]{0:T(128)S(1)} %bitcast.319, f32[128,16,64]{0,2,1:T(8,128)} %bitcast.289, f32[16,128]{1,0:T(8,128)} %get-tuple-element.33, ...), kind=kOutput, calls=%fused_computation.94 | convolution fusion | flops 203816832 | bytes 2204672 | tf_op jit(solution)/shard_map/jvp(bhts,bshp->bthp)/dot_general | solution.py:73
  203.3 18.6 %all-gather.6.cloned.1.call-done = bf16[128,8192]{0,1:T(8,128)(2,1)} async-done(((bf16[128,2048]{0,1:T(8,128)(2,1)}), bf16[128,8192]{0,1:T(8,128)(2,1)}) %all-gather.6.cloned.1.call-update) | async-done | bytes 2097168 | tf_op jit(solution)/shard_map/all_gather | solution.py:219
  221.8 6.9 %fusion = f32[128,512]{1,0:T(8,128)S(1)} fusion(bf16[128,8192]{0,1:T(8,128)(2,1)} %all-gather.6.cloned.1.call-done, bf16[1,512,8192]{2,1,0:T(8,128)(2,1)} %param.15), kind=kOutput, calls=%fused_computation.1 | convolution fusion | flops 1073741824 | bytes 10747904 | tf_op jit(solution)/shard_map/dot_general | solution.py:80
  229.1 6.3 %all-reduce.12 = (f32[128]{0:T(128)S(1)}, f32[128]{0:T(128)S(1)}) all-reduce(f32[128]{0:T(128)S(1)} %get-tuple-element.52, f32[128]{0:T(128)S(1)} %get-tuple-element.54), channel_id=1, replica_groups=mesh['section'=8,'dp'=4] {'dp'}, use_global_device_ids=true, to_apply=%region_5.6 | all-reduce | flops 256 | bytes 2048 | tf_op jit(solution)/shard_map/psum | solution.py:96
  237.4 3.3 %all-gather.8.cloned.1.call-done = bf16[128,4096]{1,0:T(8,128)(2,1)} async-done(((bf16[128,1024]{1,0:T(8,128)(2,1)}), bf16[128,4096]{1,0:T(8,128)(2,1)}) %all-gather.8.cloned.1.call-update) | async-done | bytes 1048592 | tf_op jit(solution)/shard_map/all_gather | solution.py:186
  240.7 5.9 %convolution_bitcast_fusion.1 = f32[1,4096,512]{2,1,0:T(8,128)} fusion(bf16[128,4096]{1,0:T(8,128)(2,1)} %all-gather.8.cloned.1.call-done, bf16[1,128,512]{2,1,0:T(8,128)(2,1)S(1)} %copy-done.5), kind=kOutput, calls=%fused_computation.7 | convolution fusion | flops 536870912 | bytes 9568256 | tf_op jit(solution)/shard_map/dot_general | solution.py:86
  246.7 4.3 %collective-permute-start.5 = (bf16[128,512]{1,0:T(8,128)(2,1)S(1)}, bf16[128,512]{1,0:T(8,128)(2,1)S(1)}, u32[]{:S(2)}, u32[]{:S(2)}) collective-permute-start(bf16[128,512]{1,0:T(8,128)(2,1)S(1)} %fusion.91), channel_id=1, source_target_pairs={{0,28},{4,0},{8,4},{12,8},{16,12},{20,16},{24,20},{28,24},{1,29},{... | collective-permute-start | bytes 393224 | tf_op jit(solution)/shard_map/ppermute | solution.py:29
  251.0 8.0 %all-gather.4.cloned.1.call-done = bf16[128,4096]{1,0:T(8,128)(2,1)} async-done(((bf16[128,1024]{1,0:T(8,128)(2,1)}), bf16[128,4096]{1,0:T(8,128)(2,1)}) %all-gather.4.cloned.1.call-update) | async-done | bytes 1048592 | tf_op jit(solution)/shard_map/all_gather | solution.py:177
  259.0 3.2 %fusion.17 = bf16[128,512]{1,0:T(8,128)(2,1)S(1)} fusion(bf16[128,4096]{1,0:T(8,128)(2,1)} %all-gather.4.cloned.1.call-done, bf16[1,4096,512]{2,1,0:T(8,128)(2,1)} %param.17, bf16[1,128,512]{2,1,0:T(8,128)(2,1)S(1)} %copy-done.3), kind=kOutput, calls=%fused_computation.28 | convolution fusion | flops 537067520 | bytes 5505024 | tf_op jit(solution)/shard_map/dot_general | solution.py:176
  262.2 1.5 collective-permute-start.2
  263.8 8.6 %convolution_bitcast_fusion = f32[1,512,8192]{2,1,0:T(8,128)} fusion(bf16[128,8192]{0,1:T(8,128)(2,1)S(1)} %copy-done.1, bf16[1,128,512]{2,1,0:T(8,128)(2,1)S(1)} %copy-done.2, f32[128]{0:T(128)S(1)} %copy-done.17), kind=kOutput, calls=%fused_computation | convolution fusion | flops 1073938432 | bytes 19005952 | tf_op jit(solution)/shard_map/dot_general | solution.py:86
  (161 shorter events, 27.1 us)
Async XLA Ops:
  7.2 61.8 %reduce-scatter.6.cloned.1.call-start = ((), (), s32[]{:S(2)}) async-start(), calls=%async_computation.5 | async-start | bytes 5242880 | tf_op jit(solution)/shard_map/reduce_scatter | solution.py:144
  24.1 79.6 %reduce-scatter.8.cloned.1.call-start = ((), (), s32[]{:S(2)}) async-start(), calls=%async_computation.6 | async-start | bytes 2621440 | tf_op jit(solution)/shard_map/reduce_scatter | solution.py:187
  29.9 133.4 %reduce-scatter.4.cloned.1.call-start = ((), (), s32[]{:S(2)}) async-start(), calls=%async_computation.3 | async-start | bytes 5242880 | tf_op jit(solution)/shard_map/reduce_scatter | solution.py:144
  30.3 1.5 collective-permute-start.3
  30.4 40.1 %copy-start.18 = (f32[1,1,256]{2,1,0:T(1,128)}, f32[1,1,256]{2,1,0:T(1,128)S(1)}, u32[]{:S(2)}) copy-start(f32[1,1,256]{2,1,0:T(1,128)S(1)} %get-tuple-element.43) | copy-start | bytes 3076
  30.5 40.2 %copy-start.26 = (f32[1,1,256]{2,1,0:T(1,128)}, f32[1,1,256]{2,1,0:T(1,128)S(1)}, u32[]{:S(2)}) copy-start(f32[1,1,256]{2,1,0:T(1,128)S(1)} %get-tuple-element.42) | copy-start | bytes 3076
  30.5 40.2 %copy-start.28 = (f32[1,1,256]{2,1,0:T(1,128)}, f32[1,1,256]{2,1,0:T(1,128)S(1)}, u32[]{:S(2)}) copy-start(f32[1,1,256]{2,1,0:T(1,128)S(1)} %get-tuple-element.44) | copy-start | bytes 3076
  30.5 45.7 %copy-start.24 = (f32[1,1,256]{2,1,0:T(1,128)}, f32[1,1,256]{2,1,0:T(1,128)S(1)}, u32[]{:S(2)}) copy-start(f32[1,1,256]{2,1,0:T(1,128)S(1)} %get-tuple-element.41) | copy-start | bytes 3076
  30.5 45.7 %copy-start.14 = (f32[1,1,1024]{2,1,0:T(1,128)}, f32[1,1,1024]{2,1,0:T(1,128)S(1)}, u32[]{:S(2)}) copy-start(f32[1,1,1024]{2,1,0:T(1,128)S(1)} %get-tuple-element.39) | copy-start | bytes 12292
  30.5 40.1 %copy-start.33 = (f32[16]{0:T(128)}, f32[16]{0:T(128)S(1)}, u32[]{:S(2)}) copy-start(f32[16]{0:T(128)S(1)} %negate_bitcast_fusion) | copy-start | bytes 196
  31.8 6.3 %collective-permute-start.4 = (f32[128,320]{0,1:T(8,128)S(1)}, f32[128,320]{0,1:T(8,128)S(1)}, u32[]{:S(2)}, u32[]{:S(2)}) collective-permute-start(f32[128,320]{0,1:T(8,128)S(1)} %add.241), channel_id=1, source_target_pairs={{0,2},{1,3},{2,0},{3,1},{4,6},{5,7},{6,4},{7,5},{8,10},{9,11},{10,... | collective-permute-start | bytes 491528 | tf_op jit(solution)/shard_map/ppermute | solution.py:20
  32.5 43.7 %copy-start.21 = (pred[128,128]{1,0:T(8,128)(4,1)}, pred[128,128]{1,0:T(8,128)(4,1)S(1)}, u32[]{:S(2)}) copy-start(pred[128,128]{1,0:T(8,128)(4,1)S(1)} %iota_compare_fusion) | copy-start | bytes 49156
  39.0 32.9 %copy-start.30 = (f32[16,128]{1,0:T(8,128)S(1)}, f32[16,128]{1,0:T(8,128)}, u32[]{:S(2)}) copy-start(f32[16,128]{1,0:T(8,128)} %get-tuple-element.35) | copy-start | bytes 24580
  40.8 35.4 %copy-start.6 = (bf16[1,128,256]{1,2,0:T(8,128)(2,1)}, bf16[1,128,256]{1,2,0:T(8,128)(2,1)S(1)}, u32[]{:S(2)}) copy-start(bf16[1,128,256]{1,2,0:T(8,128)(2,1)S(1)} %get-tuple-element.20) | copy-start | bytes 196612
  41.0 35.2 %copy-start.11 = (f32[128,128]{1,0:T(8,128)}, f32[128,128]{1,0:T(8,128)S(1)}, u32[]{:S(2)}) copy-start(f32[128,128]{1,0:T(8,128)S(1)} %fusion.125) | copy-start | bytes 196612
  70.6 33.2 %copy-start.13 = (f32[1,1024]{1,0:T(1,128)S(1)}, f32[1,1024]{1,0:T(1,128)}, u32[]{:S(2)}) copy-start(f32[1,1024]{1,0:T(1,128)} %param.23) | copy-start | bytes 12292
  71.9 45.7 %copy-start.8 = (f32[1,128,1024]{1,2,0:T(8,128)}, f32[1,128,1024]{1,2,0:T(8,128)S(1)}, u32[]{:S(2)}) copy-start(f32[1,128,1024]{1,2,0:T(8,128)S(1)} %get-tuple-element.22) | copy-start | bytes 1572868
  117.6 79.6 %all-reduce.16.cloned.1.call-start = ((), (), s32[]{:S(2)}) async-start(), calls=%async_computation.8 | async-start | bytes 327680 | tf_op jit(solution)/shard_map/psum | solution.py:204
  121.0 8.7 %collective-permute-start = (f32[128,320]{0,1:T(8,128)S(1)}, f32[128,320]{0,1:T(8,128)S(1)}, u32[]{:S(2)}, u32[]{:S(2)}) collective-permute-start(f32[128,320]{0,1:T(8,128)S(1)} %fusion.82), channel_id=1, source_target_pairs={{0,1},{1,0},{2,3},{3,2},{4,5},{5,4},{6,7},{7,6},{8,9},{9,8},{10,11... | collective-permute-start | bytes 491528 | tf_op jit(solution)/shard_map/ppermute | solution.py:20
  129.5 35.5 %copy-start.4 = (f32[1,128,1024]{1,2,0:T(8,128)S(1)}, f32[1,128,1024]{1,2,0:T(8,128)}, u32[]{:S(2)}) copy-start(f32[1,128,1024]{1,2,0:T(8,128)} %get-tuple-element.17) | copy-start | bytes 1572868
  129.7 6.7 %collective-permute-start.1 = (f32[128,320]{0,1:T(8,128)S(1)}, f32[128,320]{0,1:T(8,128)S(1)}, u32[]{:S(2)}, u32[]{:S(2)}) collective-permute-start(f32[128,320]{0,1:T(8,128)S(1)} %add.221), channel_id=1, source_target_pairs={{0,2},{1,3},{2,0},{3,1},{4,6},{5,7},{6,4},{7,5},{8,10},{9,11},{10,... | collective-permute-start | bytes 491528 | tf_op jit(solution)/shard_map/ppermute | solution.py:20
  138.6 83.2 %all-gather.6.cloned.1.call-start = ((), (), s32[]{:S(2)}) async-start(), calls=%async_computation.7 | async-start | bytes 2621440 | tf_op jit(solution)/shard_map/all_gather | solution.py:219
  165.0 32.2 %copy-start.19 = (f32[1,1,256]{2,1,0:T(1,128)S(1)}, f32[1,1,256]{2,1,0:T(1,128)}, u32[]{:S(2)}) copy-start(f32[1,1,256]{2,1,0:T(1,128)} %copy-done.18) | copy-start | bytes 3076
  165.0 33.2 %copy-start.25 = (f32[1,1,256]{2,1,0:T(1,128)S(1)}, f32[1,1,256]{2,1,0:T(1,128)}, u32[]{:S(2)}) copy-start(f32[1,1,256]{2,1,0:T(1,128)} %copy-done.24) | copy-start | bytes 3076
  167.6 30.7 %copy-start.29 = (f32[1,1,256]{2,1,0:T(1,128)S(1)}, f32[1,1,256]{2,1,0:T(1,128)}, u32[]{:S(2)}) copy-start(f32[1,1,256]{2,1,0:T(1,128)} %copy-done.28) | copy-start | bytes 3076
  167.6 32.1 %copy-start.23 = (pred[128,128]{1,0:T(8,128)(4,1)S(1)}, pred[128,128]{1,0:T(8,128)(4,1)}, u32[]{:S(2)}) copy-start(pred[128,128]{1,0:T(8,128)(4,1)} %copy-done.21) | copy-start | bytes 49156
  167.6 32.1 %copy-start.39 = (f32[1,16]{1,0:T(1,128)S(1)}, f32[1,16]{1,0:T(1,128)}, u32[]{:S(2)}) copy-start(f32[1,16]{1,0:T(1,128)} %param.22) | copy-start | bytes 196
  169.9 70.7 %all-gather.8.cloned.1.call-start = ((), (), s32[]{:S(2)}) async-start(), calls=%async_computation.9 | async-start | bytes 1310720 | tf_op jit(solution)/shard_map/all_gather | solution.py:186
  170.5 88.5 %all-gather.4.cloned.1.call-start = ((), (), s32[]{:S(2)}) async-start(), calls=%async_computation.4 | async-start | bytes 1310720 | tf_op jit(solution)/shard_map/all_gather | solution.py:177
  203.3 33.0 %copy-start.17 = (f32[128]{0:T(128)S(1)}, f32[128]{0:T(128)}, u32[]{:S(2)}) copy-start(f32[128]{0:T(128)} %copy-done.16) | copy-start | bytes 1540
  246.7 25.6 %collective-permute-start.5 = (bf16[128,512]{1,0:T(8,128)(2,1)S(1)}, bf16[128,512]{1,0:T(8,128)(2,1)S(1)}, u32[]{:S(2)}, u32[]{:S(2)}) collective-permute-start(bf16[128,512]{1,0:T(8,128)(2,1)S(1)} %fusion.91), channel_id=1, source_target_pairs={{0,28},{4,0},{8,4},{12,8},{16,12},{20,16},{24,20},{28,24},{1,29},{... | collective-permute-start | bytes 393224 | tf_op jit(solution)/shard_map/ppermute | solution.py:29
  262.2 10.1 %collective-permute-start.2 = (bf16[128,512]{1,0:T(8,128)(2,1)S(1)}, bf16[128,512]{1,0:T(8,128)(2,1)S(1)}, u32[]{:S(2)}, u32[]{:S(2)}) collective-permute-start(bf16[128,512]{1,0:T(8,128)(2,1)S(1)} %fusion.17), channel_id=1, source_target_pairs={{0,4},{4,8},{8,12},{12,16},{16,20},{20,24},{24,28},{28,0},{1,5},{5... | collective-permute-start | bytes 393224 | tf_op jit(solution)/shard_map/ppermute | solution.py:29
  (21 other events, 203.3 us)
Sparse Core Ops, SparseCore 0:
  24.2 44.8 reduce-scatter.5
  72.3 31.4 reduce-scatter.7
  117.7 45.6 reduce-scatter.3
  165.6 31.5 all-reduce.15
  199.2 22.5 all-gather.5
  223.8 16.8 all-gather.7
  242.2 16.7 all-gather.3
